TPU v7x, 32 devices: a whole 2x2x4 slice. The times are simulated.
32 devices in a mesh: orb: 16 (over z, x, core), tm: 2 (over y).
Axes of the slice: x: 2, y: 2, z: 4, core: 2. Of those that a mesh axis runs over, the one named last changes fastest.
Arguments:
- integrals: bfloat16 [2048, 128, 128], P('orb'), may hold values from -6 to 6
- block_map: int32 [128, 4], P('orb'), may hold values 0 or 1
- green_occ: bfloat16 [2, 2048, 384], P('tm', 'orb'), may hold values from -0.5 to 0.5
- green_virt: bfloat16 [2, 2048, 384], P('tm', 'orb'), may hold values from -0.5 to 0.5
- coulomb: bfloat16 [2048, 512], P('orb'), may hold values from -0.0048828125 to 0.0048828125
- cosine: float32 [2, 2], replicated, may hold values from -1 to 1
Outputs:
- spectrum: float32 [2, 2048, 512], P('tm', 'orb')
All inputs are finite; a program needn't handle non-finite values. No bound on the sum of `block_map` on one device may be relied on, other than what follows from the above.
Results may differ from a plain program's by a relative error of at most 0.0057.
Values may be sent and summed in bfloat16 or wider, within the bound.
A program may use at most 128 MiB of HBM per device.

v0:
```python
import jax
import jax.numpy as jnp
from jax import lax
from jax.sharding import PartitionSpec as P


def padded(value, sides, width):
    for axis, dim in sides:
        size, length = (lax.axis_size(axis), value.shape[dim])
        up = [(i, (i + 1) % size) for i in range(size)]
        down = [(j, i) for i, j in up]
        last = lax.slice_in_dim(value, length - width, length, axis=dim)
        first = lax.slice_in_dim(value, 0, width, axis=dim)
        before = lax.ppermute(last, axis, up)
        after = lax.ppermute(first, axis, down)
        value = jnp.concatenate([before, value, after], axis=dim)
    return value


def body(integrals, block_map, green_occ, green_virt, coulomb, cosine):
    aux_rows = integrals.shape[0]
    orb_count = integrals.shape[1]
    row_blocks = block_map.shape[0]
    col_blocks = block_map.shape[1]
    pair_count = orb_count * orb_count
    keep_mask = block_map.astype(jnp.bfloat16)[:, None, :, None, None]
    shaped = integrals.reshape(
        row_blocks, aux_rows // row_blocks, col_blocks, orb_count // col_blocks, orb_count
    )
    masked = (shaped * keep_mask).reshape(aux_rows, pair_count)
    packed = jnp.concatenate([masked, coulomb], axis=1)
    extended = padded(packed, (("orb", 0),), aux_rows)
    sources = [extended[:aux_rows], packed, extended[2 * aux_rows :]]
    occ_tiles = green_occ[0].reshape(orb_count, 3, orb_count)
    virt_tiles = green_virt[0].reshape(orb_count, 3, orb_count)
    running_sum = jnp.zeros((aux_rows, coulomb.shape[1]), jnp.float32)
    for offset in range(3):
        source = sources[offset]
        other_side = source[:, :pair_count].reshape(aux_rows, orb_count, orb_count)
        other_coulomb = source[:, pair_count:]
        half_side = jnp.einsum(
            "qls,ns->qln", other_side, virt_tiles[:, offset, :], preferred_element_type=jnp.float32
        ).astype(jnp.bfloat16)
        pair_side = jnp.einsum(
            "ml,qln->qmn", occ_tiles[:, offset, :], half_side, preferred_element_type=jnp.float32
        ).astype(jnp.bfloat16)
        response = lax.dot_general(
            masked,
            pair_side.reshape(aux_rows, pair_count),
            (((1,), (1,)), ((), ())),
            preferred_element_type=jnp.float32,
        ).astype(jnp.bfloat16)
        running_sum = running_sum + jnp.dot(
            response, other_coulomb, preferred_element_type=jnp.float32
        )
    time_panel = running_sum.astype(jnp.bfloat16)
    all_times = lax.all_gather(time_panel[None], "tm", axis=0, tiled=True)
    weight_row = lax.dynamic_slice_in_dim(cosine, lax.axis_index("tm"), 1, 0)
    result = jnp.einsum(
        "ft,tpk->fpk", weight_row, all_times.astype(jnp.float32), precision=lax.Precision.HIGHEST
    )
    return result


def solution(mesh):
    in_specs = (
        P("orb", None, None),
        P("orb", None),
        P("tm", "orb", None),
        P("tm", "orb", None),
        P("orb", None),
        P(),
    )
    out_specs = P("tm", "orb", None)
    return jax.shard_map(body, mesh=mesh, in_specs=in_specs, out_specs=out_specs, check_vma=False)
```

profile of v0, /device:TPU:1, one launch (start us, length us, event | category | flops | bytes accessed | tf_op | source)
XLA Modules:
  0.0 172.4 jit_solution(15324073672905840063)
XLA Ops:
  0.0 0.0 copy-start
  0.0 0.7 convert_element_type.43
  0.7 0.1 copy.9
  0.8 2.8 %mul.27 = bf16[8,16,4,32,128]{4,3,2,1,0:T(8,128)(2,1)} broadcast(bf16[8,4]{1,0:T(8,128)(2,1)S(1)} %copy.9), dimensions={0,2} | broadcast | bytes 4194368 | tf_op jit(solution)/shard_map/mul | solution.py:30
  3.6 7.3 %mul.28 = bf16[128,16384]{1,0:T(8,128)(2,1)} reshape(bf16[8,16,4,32,128]{4,3,2,1,0:T(8,128)(2,1)} %mul.27) | data formatting | bytes 8388608 | tf_op jit(solution)/shard_map/mul | solution.py:30
  11.0 0.0 copy-start.1
  11.0 6.0 %bitcast_multiply_fusion = bf16[128,16384]{1,0:T(8,128)(2,1)S(1)} fusion(bf16[128,16384]{1,0:T(8,128)(2,1)} %mul.28, bf16[16,8,128,128]{3,2,1,0:T(8,128)(2,1)} %bitcast.84), kind=kLoop, calls=%fused_computation.1 | loop fusion | flops 2097152 | bytes 12582912 | tf_op jit(solution)/shard_map/mul | solution.py:30
  17.0 0.0 copy-done.1
  17.0 0.0 copy-start.2
  17.0 0.0 copy-start.3
  17.0 2.3 %pad_maximum_fusion = bf16[128,16896]{1,0:T(8,128)(2,1)} fusion(bf16[128,512]{1,0:T(8,128)(2,1)S(1)} %copy-done.1, bf16[128,16384]{1,0:T(8,128)(2,1)S(1)} %bitcast_multiply_fusion), kind=kLoop, calls=%fused_computation | loop fusion | flops 8650752 | bytes 8650752 | tf_op jit(solution)/shard_map/concatenate | solution.py:31
  19.3 0.0 collective-permute-start.1
  19.3 2.6 %collective-permute-start = (bf16[128,16896]{1,0:T(8,128)(2,1)}, bf16[128,16896]{1,0:T(8,128)(2,1)}, u32[]{:S(2)}, u32[]{:S(2)}) collective-permute-start(bf16[128,16896]{1,0:T(8,128)(2,1)} %pad_maximum_fusion), channel_id=1, source_target_pairs={{0,2},{2,4},{4,6},{6,8},{8,10},{10,12},{12,14},{14,16},{16,18},{18... | collective-permute-start | bytes 12976136 | tf_op jit(solution)/shard_map/ppermute | solution.py:14
  21.9 0.0 copy-done.2
  21.9 0.1 copy.11
  22.0 0.0 copy-done.3
  22.1 0.1 copy.13
  22.2 0.1 mul.23
  22.3 0.1 mul.24
  22.4 5.8 %broadcast_multiply_fusion = bf16[128,128,128]{2,1,0:T(8,128)(2,1)} fusion(bf16[128,128,128]{2,1,0:T(8,128)(2,1)} %param.6, bf16[128,128]{1,0:T(8,128)(2,1)S(1)} %mul.24), kind=kLoop, calls=%fused_computation.22 | loop fusion | flops 2097152 | bytes 8421376 | tf_op jit(solution)/shard_map/mul | solution.py:30
  28.2 5.7 %convert_bitcast_fusion.1 = bf16[128,128,128]{1,2,0:T(8,128)(2,1)} fusion(bf16[128,128,128]{2,1,0:T(8,128)(2,1)} %broadcast_multiply_fusion, bf16[128,3,128]{0,2,1:T(8,128)(2,1)S(1)} %bitcast.90, bf16[128,3,128]{0,2,1:T(8,128)(2,1)S(1)} %bitcast.87), kind=kOutput, calls=%fused_computation.7 | convolution fusion | flops 1077936128 | bytes 8454144 | tf_op jit(solution)/shard_map/ml,qln->qmn/dot_general | solution.py:44
  33.9 7.2 %copy.21 = bf16[128,128,128]{0,2,1:T(8,128)(2,1)} copy(bf16[128,128,128]{1,2,0:T(8,128)(2,1)} %convert_bitcast_fusion.1) | data formatting | bytes 8388608 | tf_op jit(solution)/shard_map/convert_element_type | solution.py:46
  41.2 6.2 %fusion.45 = f32[128,512]{1,0:T(8,128)S(1)} fusion(bf16[128,512]{1,0:T(8,128)(2,1)S(1)} %copy-done.1, bf16[128,128,128]{0,2,1:T(8,128)(2,1)} %copy.21, bf16[128,128,128]{2,1,0:T(8,128)(2,1)} %broadcast_multiply_fusion), kind=kOutput, calls=%fused_computation.32 | convolution fusion | flops 553664512 | bytes 8781824 | tf_op jit(solution)/shard_map/dot_general | solution.py:53
  47.4 68.7 %collective-permute-done.1 = bf16[128,16896]{1,0:T(8,128)(2,1)} collective-permute-done((bf16[128,16896]{1,0:T(8,128)(2,1)}, bf16[128,16896]{1,0:T(8,128)(2,1)}, u32[]{:S(2)}, u32[]{:S(2)}) %collective-permute-start.1) | collective-permute-done | bytes 4325408 | tf_op jit(solution)/shard_map/ppermute | solution.py:15
  116.2 2.5 %slice_bitcast_fusion = bf16[16,8,128,128]{3,1,2,0:T(8,128)(2,1)S(1)} fusion(bf16[128,16896]{1,0:T(8,128)(2,1)} %collective-permute-done.1), kind=kLoop, calls=%fused_computation.2 | loop fusion | bytes 8388608
  118.7 3.2 %copy.27 = bf16[16,8,128,128]{3,2,1,0:T(8,128)(2,1)} copy(bf16[16,8,128,128]{3,1,2,0:T(8,128)(2,1)S(1)} %slice_bitcast_fusion) | data formatting | bytes 8388608
  121.9 5.8 %convert_bitcast_fusion = bf16[128,128,128]{1,2,0:T(8,128)(2,1)} fusion(bf16[128,128,128]{2,1,0:T(8,128)(2,1)} %bitcast.86, bf16[128,3,128]{0,2,1:T(8,128)(2,1)S(1)} %bitcast.91, bf16[128,3,128]{0,2,1:T(8,128)(2,1)S(1)} %bitcast.88), kind=kOutput, calls=%fused_computation.4 | convolution fusion | flops 1077936128 | bytes 8454144 | tf_op jit(solution)/shard_map/ml,qln->qmn/dot_general | solution.py:44
  127.7 7.3 %copy.22 = bf16[128,128,128]{0,2,1:T(8,128)(2,1)} copy(bf16[128,128,128]{1,2,0:T(8,128)(2,1)} %convert_bitcast_fusion) | data formatting | bytes 8388608 | tf_op jit(solution)/shard_map/convert_element_type | solution.py:46
  134.9 0.0 collective-permute-done
  134.9 2.5 %slice_bitcast_fusion.1 = bf16[16,8,128,128]{3,1,2,0:T(8,128)(2,1)S(1)} fusion(bf16[128,16896]{1,0:T(8,128)(2,1)} %collective-permute-done), kind=kLoop, calls=%fused_computation.3 | loop fusion | bytes 8388608
  137.4 3.2 %copy.26 = bf16[16,8,128,128]{3,2,1,0:T(8,128)(2,1)} copy(bf16[16,8,128,128]{3,1,2,0:T(8,128)(2,1)S(1)} %slice_bitcast_fusion.1) | data formatting | bytes 8388608
  140.6 5.8 %convert_bitcast_fusion.2 = bf16[128,128,128]{1,2,0:T(8,128)(2,1)} fusion(bf16[128,128,128]{2,1,0:T(8,128)(2,1)} %bitcast.85, bf16[128,3,128]{0,2,1:T(8,128)(2,1)S(1)} %bitcast.92, bf16[128,3,128]{0,2,1:T(8,128)(2,1)S(1)} %bitcast.89), kind=kOutput, calls=%fused_computation.10 | convolution fusion | flops 1077936128 | bytes 8454144 | tf_op jit(solution)/shard_map/ml,qln->qmn/dot_general | solution.py:44
  146.4 7.3 %copy.20 = bf16[128,128,128]{0,2,1:T(8,128)(2,1)} copy(bf16[128,128,128]{1,2,0:T(8,128)(2,1)} %convert_bitcast_fusion.2) | data formatting | bytes 8388608 | tf_op jit(solution)/shard_map/convert_element_type | solution.py:46
  153.7 6.2 %fusion.39 = f32[128,512]{1,0:T(8,128)S(1)} fusion(bf16[128,128,128]{0,2,1:T(8,128)(2,1)} %copy.22, bf16[128,128,128]{2,1,0:T(8,128)(2,1)} %broadcast_multiply_fusion, bf16[128,16896]{1,0:T(8,128)(2,1)} %collective-permute-done.1), kind=kOutput, calls=%fused_computation.30 | convolution fusion | flops 553664512 | bytes 8781824 | tf_op jit(solution)/shard_map/dot_general | solution.py:53
  159.9 6.2 %fusion.25 = bf16[128,512]{1,0:T(8,128)(2,1)S(1)} fusion(f32[128,512]{1,0:T(8,128)S(1)} %fusion.39, f32[128,512]{1,0:T(8,128)S(1)} %fusion.45, bf16[128,128,128]{0,2,1:T(8,128)(2,1)} %copy.20, bf16[128,128,128]{2,1,0:T(8,128)(2,1)} %broadcast_multiply_fusion, bf16[128,16896]{1,0:T(8,128)(2,1)} %collective-permute-done), kind=kOutput, calls=%fused_computation.25 | convolution fusion | flops 553861120 | bytes 9175040 | tf_op jit(solution)/shard_map/dot_general | solution.py:53
  166.2 4.5 %all-gather = bf16[256,512]{1,0:T(8,128)(2,1)S(1)} all-gather(bf16[128,512]{1,0:T(8,128)(2,1)S(1)} %fusion.25), channel_id=2, replica_groups=mesh['orb'=16,'tm'=2] {'tm'}, dimensions={0}, use_global_device_ids=true | all-gather | bytes 393216 | tf_op jit(solution)/shard_map/all_gather | solution.py:57
  170.7 0.0 copy-done
  170.7 1.0 fusion.52
  171.7 0.7 copy.24
Async XLA Ops:
  0.0 170.7 %copy-start = (f32[2,2]{1,0:T(2,128)S(1)}, f32[2,2]{1,0:T(2,128)}, u32[]{:S(2)}) copy-start(f32[2,2]{1,0:T(2,128)} %param.11) | copy-start | bytes 52
  11.0 6.0 %copy-start.1 = (bf16[128,512]{1,0:T(8,128)(2,1)S(1)}, bf16[128,512]{1,0:T(8,128)(2,1)}, u32[]{:S(2)}) copy-start(bf16[128,512]{1,0:T(8,128)(2,1)} %param.10) | copy-start | bytes 393220
  17.0 4.9 %copy-start.2 = (bf16[1,128,384]{2,1,0:T(8,128)(2,1)S(1)}, bf16[1,128,384]{2,1,0:T(8,128)(2,1)}, u32[]{:S(2)}) copy-start(bf16[1,128,384]{2,1,0:T(8,128)(2,1)} %param.9) | copy-start | bytes 294916
  17.0 5.1 %copy-start.3 = (bf16[1,128,384]{2,1,0:T(8,128)(2,1)S(1)}, bf16[1,128,384]{2,1,0:T(8,128)(2,1)}, u32[]{:S(2)}) copy-start(bf16[1,128,384]{2,1,0:T(8,128)(2,1)} %param.8) | copy-start | bytes 294916
  19.3 96.8 %collective-permute-start.1 = (bf16[128,16896]{1,0:T(8,128)(2,1)}, bf16[128,16896]{1,0:T(8,128)(2,1)}, u32[]{:S(2)}, u32[]{:S(2)}) collective-permute-start(bf16[128,16896]{1,0:T(8,128)(2,1)} %pad_maximum_fusion), channel_id=1, source_target_pairs={{2,0},{4,2},{6,4},{8,6},{10,8},{12,10},{14,12},{16,14},{18,16},{20... | collective-permute-start | bytes 12976136 | tf_op jit(solution)/shard_map/ppermute | solution.py:15
  19.3 115.6 %collective-permute-start = (bf16[128,16896]{1,0:T(8,128)(2,1)}, bf16[128,16896]{1,0:T(8,128)(2,1)}, u32[]{:S(2)}, u32[]{:S(2)}) collective-permute-start(bf16[128,16896]{1,0:T(8,128)(2,1)} %pad_maximum_fusion), channel_id=1, source_target_pairs={{0,2},{2,4},{4,6},{6,8},{8,10},{10,12},{12,14},{14,16},{16,18},{18... | collective-permute-start | bytes 12976136 | tf_op jit(solution)/shard_map/ppermute | solution.py:14
where the time goes:
time: 173 us; the launch traced here: 172 us
  waiting for transfers between devices  68.7 us (40%)
  local copies, waits for them, and re-layouts  44.6 us (26%)
  matrix products  37 us (21%)
  other arithmetic  14.8 us (9%)
  blocking collectives  4.48 us (3%)
  starting transfers between devices  2.59 us (1%)
    ppermute x1, waiting for transfers between devices, padded(): after = lax.ppermute(first, axis, down)  68.7 us
    convert_element_type x3, local copies, waits for them, and re-layouts, body(): pair_side = jnp.einsum('ml,qln->qmn', occ_tiles[:, offset, :], half_side,...  21.8 us
    dot_general x3, matrix products, body(): jnp.dot(response, other_coulomb, preferred_element_type=jnp.float32)  18.7 us
    dot_general x3, matrix products, body(): jnp.einsum('ml,qln->qmn', occ_tiles[:, offset, :], half_side, preferred_e...  17.3 us
    mul x2, other arithmetic, body(): masked = (shaped * keep_mask).reshape(aux_rows, pair_count)  11.8 us
    unnamed x14, local copies, waits for them, and re-layouts  11.7 us
    mul x4, local copies, waits for them, and re-layouts, body(): masked = (shaped * keep_mask).reshape(aux_rows, pair_count)  10.4 us
    all_gather x1, blocking collectives, body(): all_times = lax.all_gather(time_panel[None], 'tm', axis=0, tiled=True)  4.48 us
  transfers between devices with their start and end apart: 2, of which 1 were waited for; matrix products, arithmetic and copies ran while one was open for 26% of the time, Pallas kernels for 0%

commit v1 on v0

v1 whole, which is shorter than its diff:
```python
import functools

import jax
import jax.numpy as jnp
from jax import lax
from jax.experimental import pallas as pl
from jax.experimental.pallas import tpu as pltpu
from jax.sharding import PartitionSpec as P

MESH = pl.DeviceIdType.MESH
BF = jnp.bfloat16
F32 = jnp.float32


def mm(a, b):
    return jnp.dot(a, b, preferred_element_type=F32)


def mm_nt(a, b):
    return lax.dot_general(a, b, (((1,), (1,)), ((), ())), preferred_element_type=F32)


def mm_tn(a, b):
    return lax.dot_general(a, b, (((0,), (0,)), ((), ())), preferred_element_type=F32)


def flip(tile):
    return tile.astype(F32).T.astype(BF)


def kernel(
    chain, times, chunk, group,
    ints, bmap, occ, virt, coul, cosine, out,
    own, xbuf, bmap_left, mask, mask_left, occ_all, virt_all, occ_left, virt_left,
    coul_left, coul_right, w_diag, w_left, w_back, l_diag, l_left, l_back,
    stage, rel, own_rel, acc, z_send, z_recv,
    own_sem, x_send, x_recv, small_send, small_recv, tile_send, tile_recv,
    edge_send, edge_recv, zs_send, zs_recv,
):
    aux, orb = ints.shape[0], ints.shape[1]
    part = aux // times
    chunks = part // chunk
    groups = chunk // group
    row_blocks, col_blocks = bmap.shape
    width = orb // col_blocks
    me = lax.axis_index("orb")
    y = lax.axis_index("tm")
    right = lax.rem(me + 1, chain)
    left = lax.rem(me + chain - 1, chain)
    peers = [lax.rem(y + d, times) for d in range(times)]

    barrier = pltpu.get_barrier_semaphore()
    for d in range(times):
        for where in (left, right) + ((me,) if d else ()):
            pl.semaphore_signal(
                barrier, inc=1, device_id=(where, peers[d]), device_id_type=MESH
            )

    loads = []
    for i in range(aux // chunk):
        rows = pl.ds(i * chunk, chunk)
        loads.append(pltpu.make_async_copy(ints.at[rows], own.at[rows], own_sem.at[i]))
        loads[-1].start()
    pl.semaphore_wait(barrier, 3 * times - 1)

    def send(src, dst, s, r, where, peer):
        copy = pltpu.make_async_remote_copy(
            src_ref=src, dst_ref=dst, send_sem=s, recv_sem=r,
            device_id=(where, peer), device_id_type=MESH,
        )
        copy.start()
        return copy

    near = pl.ds(0, 2 * orb)
    far = pl.ds(2 * orb, orb)
    tiles = []
    for d in range(1, times):
        for k, (src, dst) in enumerate(((occ, occ_all), (virt, virt_all))):
            tiles.append(send(
                src.at[0, :, near], dst.at[y],
                tile_send.at[d, k], tile_recv.at[d, k], me, peers[d],
            ))
    edges = []
    for d in range(times):
        for k, (src, dst) in enumerate(((occ, occ_left), (virt, virt_left))):
            edges.append(send(
                src.at[0, :, far], dst.at[y],
                edge_send.at[d, k], edge_recv.at[d, k], right, peers[d],
            ))
    small = [send(bmap, bmap_left, small_send.at[0], small_recv.at[0], right, y)]
    blocks = []
    for c in range(chunks):
        blocks.append(send(
            ints.at[pl.ds(y * part + c * chunk, chunk)], xbuf.at[pl.ds(c * chunk, chunk)],
            x_send.at[c], x_recv.at[c], right, y,
        ))
    small.append(send(coul, coul_left, small_send.at[1], small_recv.at[1], right, y))
    small.append(send(coul, coul_right, small_send.at[2], small_recv.at[2], left, y))

    def build_mask(src, dst):
        values = src[...].astype(F32)
        for r in range(row_blocks):
            for c in range(col_blocks):
                dst[r, pl.ds(c * width, width), :] = jnp.broadcast_to(
                    values[r : r + 1, c : c + 1], (width, orb)
                ).astype(BF)

    build_mask(bmap, mask)
    occ_all[y] = occ[0, :, : 2 * orb]
    virt_all[y] = virt[0, :, : 2 * orb]
    for load in loads:
        load.wait()

    per_block = aux // row_blocks

    def arrange(g, carry):
        r = g * group // per_block
        for b in range(orb // group):
            tile = own[pl.ds(g * group, group), pl.ds(b * group, group), :]
            tile = jnp.swapaxes(tile * mask[r, pl.ds(b * group, group), :][None], 0, 1)
            for j in range(0, group, 2):
                own_rel[(b * group + j) // 2, g] = jnp.concatenate(
                    [tile[j], tile[j + 1]], axis=1
                )
        return carry

    lax.fori_loop(0, aux // group, arrange, 0)

    def transform(src, base, keep, first, weights, lefts, slot):
        held = keep[(first + base) // per_block]
        for quad in range(0, group, 4):
            x = src[pl.ds(base + quad, 4)] * held[None]
            half = mm(x.reshape(4 * orb, orb), weights[...]).astype(BF)
            for t in range(times):
                columns = [
                    half[q * orb : (q + 1) * orb, t * orb : (t + 1) * orb] for q in range(4)
                ]
                pair = mm(lefts[t], jnp.concatenate(columns, axis=1)).astype(BF)
                for q in range(4):
                    stage[t, quad + q] = pair[:, q * orb : (q + 1) * orb]
        for t in range(times):
            for b in range(orb // group):
                rel[pl.ds(b * group, group), slot(t)] = jnp.swapaxes(
                    stage[t, :, pl.ds(b * group, group), :], 0, 1
                )

    def respond(count):
        acc[...] = jnp.zeros_like(acc)

        def step(i, carry):
            total = jnp.zeros((count * group, aux), F32)
            for u in range(4):
                m = i * 4 + u
                a = jnp.concatenate(
                    [rel[2 * m + k, :count].reshape(count * group, orb) for k in range(2)], axis=1
                )
                total = total + mm_nt(a, own_rel[m].reshape(aux, 2 * orb))
            acc[: count * group] += total
            return carry

        lax.fori_loop(0, orb // 8, step, 0)

    def combine(f, first, rows):
        total = cosine[f, 0] * acc[pl.ds(first, rows)]
        for t in range(1, times):
            total = total + cosine[f, t] * acc[pl.ds(first + t * rows, rows)]
        return total.astype(BF)

    for copy in tiles:
        copy.wait()
    for t in range(times):
        lanes = pl.ds(t * orb, orb)
        w_left[:, lanes] = flip(virt_all[t, :, :orb])
        w_diag[:, lanes] = flip(virt_all[t, :, orb:])
        l_left[t] = occ_all[t, :, :orb]
        l_diag[t] = occ_all[t, :, orb:]

    own_groups = part // group

    def diagonal(g, carry):
        transform(
            own, y * part + g * group, mask, 0, w_diag, l_diag, lambda t: t * own_groups + g
        )
        return carry

    lax.fori_loop(0, own_groups, diagonal, 0)
    respond(times * own_groups)
    for f in range(times):
        z_send[f, 0] = combine(f, 0, part)

    for copy in edges:
        copy.wait()
    for t in range(times):
        w_back[:, pl.ds(t * orb, orb)] = virt_left[t]
        l_back[t] = flip(occ_left[t])
    small[0].wait()
    build_mask(bmap_left, mask_left)

    for c in range(chunks):
        blocks[c].wait()

        def both(g, carry, c=c):
            base = c * chunk + g * group
            transform(
                xbuf, base, mask_left, y * part, w_left, l_left, lambda t: t * groups + g
            )
            transform(
                xbuf, base, mask_left, y * part, w_back, l_back,
                lambda t: (times + t) * groups + g,
            )
            return carry

        lax.fori_loop(0, groups, both, 0)
        respond(2 * times * groups)
        for f in range(times):
            rows = pl.ds(c * chunk, chunk)
            z_send[f, 1, rows] = combine(f, 0, chunk)
            z_send[f, 2, rows] = combine(f, times * chunk, chunk)

    z_copies = []
    for d in range(times):
        z_copies.append(send(
            z_send.at[peers[d], 2], z_recv.at[2, y], zs_send.at[1, d], zs_recv.at[1, d],
            left, peers[d],
        ))
        if d:
            z_copies.append(send(
                z_send.at[peers[d], pl.ds(0, 2)], z_recv.at[pl.ds(0, 2), y],
                zs_send.at[0, d], zs_recv.at[0, d], me, peers[d],
            ))
    z_recv[0, y] = z_send[y, 0]
    z_recv[1, y] = z_send[y, 1]
    for copy in small[1:] + z_copies:
        copy.wait()

    result = mm_tn(z_recv[0].reshape(aux, aux), coul[...])
    result = result + mm_tn(z_recv[1].reshape(aux, aux), coul_left[...])
    out[0] = result + mm(z_recv[2].reshape(aux, aux), coul_right[...])


def solution(mesh):
    chain, times = mesh.shape["orb"], mesh.shape["tm"]

    def body(integrals, block_map, green_occ, green_virt, coulomb, cosine):
        aux, orb = integrals.shape[0], integrals.shape[1]
        kw = coulomb.shape[1]
        part = aux // times
        group = aux // block_map.shape[0]
        chunk = min(2 * group, part)
        count = max(part, 2 * chunk) * times // group
        vmem = pl.BlockSpec(memory_space=pltpu.VMEM)
        dma = pltpu.SemaphoreType.DMA
        scratch = [
            pltpu.VMEM((aux, orb, orb), BF),
            pltpu.VMEM((part, orb, orb), BF),
            pltpu.VMEM(block_map.shape, jnp.int32),
            pltpu.VMEM((block_map.shape[0], orb, orb), BF),
            pltpu.VMEM((block_map.shape[0], orb, orb), BF),
            pltpu.VMEM((times, orb, 2 * orb), BF),
            pltpu.VMEM((times, orb, 2 * orb), BF),
            pltpu.VMEM((times, orb, orb), BF),
            pltpu.VMEM((times, orb, orb), BF),
            pltpu.VMEM((aux, kw), BF),
            pltpu.VMEM((aux, kw), BF),
            pltpu.VMEM((orb, times * orb), BF),
            pltpu.VMEM((orb, times * orb), BF),
            pltpu.VMEM((orb, times * orb), BF),
            pltpu.VMEM((times, orb, orb), BF),
            pltpu.VMEM((times, orb, orb), BF),
            pltpu.VMEM((times, orb, orb), BF),
            pltpu.VMEM((times, group, orb, orb), BF),
            pltpu.VMEM((orb, count, group, orb), BF),
            pltpu.VMEM((orb // 2, aux // group, group, 2 * orb), BF),
            pltpu.VMEM((count * group, aux), F32),
            pltpu.VMEM((times, 3, part, aux), BF),
            pltpu.VMEM((3, times, part, aux), BF),
            dma((aux // chunk,)),
            dma((part // chunk,)), dma((part // chunk,)),
            dma((3,)), dma((3,)),
            dma((times, 2)), dma((times, 2)),
            dma((times, 2)), dma((times, 2)),
            dma((2, times)), dma((2, times)),
        ]
        return pl.pallas_call(
            functools.partial(kernel, chain, times, chunk, group),
            out_shape=jax.ShapeDtypeStruct((1, aux, kw), F32),
            in_specs=[
                pl.BlockSpec(memory_space=pl.ANY), vmem, vmem, vmem, vmem,
                pl.BlockSpec(memory_space=pltpu.SMEM),
            ],
            out_specs=vmem,
            scratch_shapes=scratch,
            compiler_params=pltpu.CompilerParams(
                collective_id=0, has_side_effects=True, vmem_limit_bytes=56 * 2**20
            ),
        )(integrals, block_map, green_occ, green_virt, coulomb, cosine)

    in_specs = (
        P("orb", None, None),
        P("orb", None),
        P("tm", "orb", None),
        P("tm", "orb", None),
        P("orb", None),
        P(),
    )
    out_specs = P("tm", "orb", None)
    return jax.shard_map(body, mesh=mesh, in_specs=in_specs, out_specs=out_specs, check_vma=False)
```

time: 173 us -> 47.8 us (0.28)
  the two profiles are of different devices: /device:TPU:1 before, /device:TPU:0 now
where the time goes in v1:
time: 47.8 us; the launch traced here: 47.6 us
  Pallas kernels  44.6 us (93%)
  local copies, waits for them, and re-layouts  3.02 us (6%)
    pallas_call x1, Pallas kernels, body(): pl.pallas_call(functools.partial(kernel, chain, times, chunk, group), out...  44.6 us
    unnamed x2, local copies, waits for them, and re-layouts  3.02 us

profile of v1, /device:TPU:0, one launch (start us, length us, event | category | flops | bytes accessed | tf_op | source)
XLA Modules:
  0.0 47.6 jit_solution(6860644972512801311)
XLA Ops:
  0.0 1.3 %copy.7.bmap = s32[8,4]{1,0:T(8,128)} copy(s32[8,4]{0,1:T(4,128)} %param.7) | data formatting | bytes 256 | tf_op args[1]
  1.3 44.6 %shard_map.64 = f32[1,128,512]{2,1,0:T(8,128)} custom-call(bf16[128,128,128]{2,1,0:T(8,128)(2,1)} %ints.1, s32[8,4]{1,0:T(8,128)} %copy.7.bmap, bf16[1,128,384]{2,1,0:T(8,128)(2,1)} %occ.1, bf16[1,128,384]{2,1,0:T(8,128)(2,1)} %virt.1, bf16[128,512]{1,0:T(8,128)(2,1)} %coul.1, f32[2,2]{1,0:T(2,128)} %cosine.1), custom_call_target="tpu_custom_call" | custom-call | tf_op jit(solution)/shard_map/pallas_call | solution.py:284
  45.9 1.7 %copy.9 = f32[1,128,512]{2,1,0:T(8,128)} copy(f32[1,128,512]{2,1,0:T(8,128)} %shard_map.64) | data formatting | bytes 524288

commit v2 on v1

--- a/solution.py
+++ b/solution.py
@@ -41,7 +41,7 @@
     part = aux // times
     chunks = part // chunk
     groups = chunk // group
-    row_blocks, col_blocks = bmap.shape
+    col_blocks, row_blocks = bmap.shape
     width = orb // col_blocks
     me = lax.axis_index("orb")
     y = lax.axis_index("tm")
@@ -81,12 +81,10 @@
                 tile_send.at[d, k], tile_recv.at[d, k], me, peers[d],
             ))
     edges = []
-    for d in range(times):
-        for k, (src, dst) in enumerate(((occ, occ_left), (virt, virt_left))):
-            edges.append(send(
-                src.at[0, :, far], dst.at[y],
-                edge_send.at[d, k], edge_recv.at[d, k], right, peers[d],
-            ))
+    for k, (src, dst) in enumerate(((occ, occ_left), (virt, virt_left))):
+        edges.append(send(
+            src.at[0, :, far], dst.at[y], edge_send.at[0, k], edge_recv.at[0, k], right, y
+        ))
     small = [send(bmap, bmap_left, small_send.at[0], small_recv.at[0], right, y)]
     blocks = []
     for c in range(chunks):
@@ -94,15 +92,13 @@
             ints.at[pl.ds(y * part + c * chunk, chunk)], xbuf.at[pl.ds(c * chunk, chunk)],
             x_send.at[c], x_recv.at[c], right, y,
         ))
-    small.append(send(coul, coul_left, small_send.at[1], small_recv.at[1], right, y))
-    small.append(send(coul, coul_right, small_send.at[2], small_recv.at[2], left, y))
 
     def build_mask(src, dst):
         values = src[...].astype(F32)
         for r in range(row_blocks):
             for c in range(col_blocks):
                 dst[r, pl.ds(c * width, width), :] = jnp.broadcast_to(
-                    values[r : r + 1, c : c + 1], (width, orb)
+                    values[c : c + 1, r : r + 1], (width, orb)
                 ).astype(BF)
 
     build_mask(bmap, mask)
@@ -112,6 +108,7 @@
         load.wait()
 
     per_block = aux // row_blocks
+    span = orb // col_blocks
 
     def arrange(g, carry):
         r = g * group // per_block
@@ -148,17 +145,19 @@
         acc[...] = jnp.zeros_like(acc)
 
         def step(i, carry):
-            total = jnp.zeros((count * group, aux), F32)
-            for u in range(4):
-                m = i * 4 + u
-                a = jnp.concatenate(
-                    [rel[2 * m + k, :count].reshape(count * group, orb) for k in range(2)], axis=1
-                )
-                total = total + mm_nt(a, own_rel[m].reshape(aux, 2 * orb))
+            a = jnp.concatenate(
+                [rel[span * i + k, :count].reshape(count * group, orb) for k in range(span)],
+                axis=1,
+            )
+            b = jnp.concatenate(
+                [own_rel[span // 2 * i + k].reshape(aux, 2 * orb) for k in range(span // 2)],
+                axis=1,
+            )
+            total = mm_nt(a, b)
             acc[: count * group] += total
             return carry
 
-        lax.fori_loop(0, orb // 8, step, 0)
+        lax.fori_loop(0, orb // span, step, 0)
 
     def combine(f, first, rows):
         total = cosine[f, 0] * acc[pl.ds(first, rows)]
@@ -167,7 +166,7 @@
         return total.astype(BF)
 
     for copy in tiles:
-        copy.wait()
+        copy.wait_recv()
     for t in range(times):
         lanes = pl.ds(t * orb, orb)
         w_left[:, lanes] = flip(virt_all[t, :, :orb])
@@ -176,6 +175,14 @@
         l_diag[t] = occ_all[t, :, orb:]
 
     own_groups = part // group
+    for copy in edges:
+        copy.wait_recv()
+    passed = []
+    for d in range(1, times):
+        for k, where in enumerate((occ_left, virt_left)):
+            passed.append(send(
+                where.at[y], where.at[y], edge_send.at[d, k], edge_recv.at[d, k], me, peers[d]
+            ))
 
     def diagonal(g, carry):
         transform(
@@ -188,16 +195,21 @@
     for f in range(times):
         z_send[f, 0] = combine(f, 0, part)
 
-    for copy in edges:
-        copy.wait()
+    for copy in passed:
+        copy.wait_recv()
     for t in range(times):
         w_back[:, pl.ds(t * orb, orb)] = virt_left[t]
         l_back[t] = flip(occ_left[t])
-    small[0].wait()
+    small[0].wait_recv()
     build_mask(bmap_left, mask_left)
 
     for c in range(chunks):
-        blocks[c].wait()
+        blocks[c].wait_recv()
+        if c == chunks - 1:
+            for block in blocks:
+                block.wait_send()
+            small.append(send(coul, coul_left, small_send.at[1], small_recv.at[1], right, y))
+            small.append(send(coul, coul_right, small_send.at[2], small_recv.at[2], left, y))
 
         def both(g, carry, c=c):
             base = c * chunk + g * group
@@ -231,11 +243,13 @@
     z_recv[0, y] = z_send[y, 0]
     z_recv[1, y] = z_send[y, 1]
     for copy in small[1:] + z_copies:
-        copy.wait()
+        copy.wait_recv()
 
     result = mm_tn(z_recv[0].reshape(aux, aux), coul[...])
     result = result + mm_tn(z_recv[1].reshape(aux, aux), coul_left[...])
     out[0] = result + mm(z_recv[2].reshape(aux, aux), coul_right[...])
+    for copy in tiles + edges + passed + small + z_copies:
+        copy.wait_send()
 
 
 def solution(mesh):
@@ -246,14 +260,14 @@
         kw = coulomb.shape[1]
         part = aux // times
         group = aux // block_map.shape[0]
-        chunk = min(2 * group, part)
+        chunk = group
         count = max(part, 2 * chunk) * times // group
         vmem = pl.BlockSpec(memory_space=pltpu.VMEM)
         dma = pltpu.SemaphoreType.DMA
         scratch = [
             pltpu.VMEM((aux, orb, orb), BF),
             pltpu.VMEM((part, orb, orb), BF),
-            pltpu.VMEM(block_map.shape, jnp.int32),
+            pltpu.VMEM(block_map.shape[::-1], jnp.int32),
             pltpu.VMEM((block_map.shape[0], orb, orb), BF),
             pltpu.VMEM((block_map.shape[0], orb, orb), BF),
             pltpu.VMEM((times, orb, 2 * orb), BF),
@@ -293,7 +307,7 @@
             compiler_params=pltpu.CompilerParams(
                 collective_id=0, has_side_effects=True, vmem_limit_bytes=56 * 2**20
             ),
-        )(integrals, block_map, green_occ, green_virt, coulomb, cosine)
+        )(integrals, block_map.T, green_occ, green_virt, coulomb, cosine)
 
     in_specs = (
         P("orb", None, None),

time: 47.8 us -> 42.2 us (0.88)
  Pallas kernels: 44.6 us -> 40.4 us
  local copies, waits for them, and re-layouts: 3.02 us -> 1.67 us
    pallas_call x1, Pallas kernels: 44.6 us -> 40.4 us  [body(): pl.pallas_call(functools.partial(kernel, chain, times, chunk, group), out...]
    unnamed x2 -> x1, local copies, waits for them, and re-layouts: 3.02 us -> 1.67 us
where the time goes in v2:
time: 42.2 us; the launch traced here: 42 us
  Pallas kernels  40.4 us (96%)
  local copies, waits for them, and re-layouts  1.67 us (4%)
    pallas_call x1, Pallas kernels, body(): pl.pallas_call(functools.partial(kernel, chain, times, chunk, group), out...  40.4 us
    unnamed x1, local copies, waits for them, and re-layouts  1.67 us

profile of v2, /device:TPU:0, one launch (start us, length us, event | category | flops | bytes accessed | tf_op | source)
XLA Modules:
  0.0 42.0 jit_solution(9290872784115088968)
XLA Ops:
  0.0 40.4 %shard_map.64 = f32[1,128,512]{2,1,0:T(8,128)} custom-call(bf16[128,128,128]{2,1,0:T(8,128)(2,1)} %ints.1, s32[4,8]{1,0:T(4,128)} %bitcast.1, bf16[1,128,384]{2,1,0:T(8,128)(2,1)} %occ.1, bf16[1,128,384]{2,1,0:T(8,128)(2,1)} %virt.1, bf16[128,512]{1,0:T(8,128)(2,1)} %coul.1, f32[2,2]{1,0:T(2,128)} %cosine.1), custom_call_target="tpu_custom_call" | custom-call | tf_op jit(solution)/shard_map/pallas_call | solution.py:298
  40.4 1.7 %copy.8 = f32[1,128,512]{2,1,0:T(8,128)} copy(f32[1,128,512]{2,1,0:T(8,128)} %shard_map.64) | data formatting | bytes 524288
